TPU v7x, 32 devices: a whole 2x2x4 slice. The times are simulated.
32 devices in a mesh: dp: 4 (over y, x), expert: 8 (over z, core).
Axes of the slice: x: 2, y: 2, z: 4, core: 2. Of those that a mesh axis runs over, the one named last changes fastest.
Arguments:
- tokens: bfloat16 [1024, 1024], P(('dp', 'expert')), may hold values from -6 to 6
- cotangent: bfloat16 [1024, 1024], P(('dp', 'expert')), may hold values from -3 to 3
- routes: int32 [1024, 8], P(('dp', 'expert')), may hold values from 0 to 7, as said below
- combine: bfloat16 [1024, 8], P(('dp', 'expert')), may hold values from 0.099609375 to 1
- hot_experts: int32 [4], replicated, may hold values from 0 to 3, as said below
- extra_slots: int32 [4], replicated, may hold values from 1 to 4, as said below
- w_gate: bfloat16 [8, 1024, 384], P('expert'), may hold values from -0.1875 to 0.1875
- w_up: bfloat16 [8, 1024, 384], P('expert'), may hold values from -0.1875 to 0.1875
- w_down: bfloat16 [8, 384, 1024], P('expert'), may hold values from -0.3125 to 0.3125
Outputs:
- token_grads: bfloat16 [1024, 1024], P(('dp', 'expert'))
- grad_gate: bfloat16 [8, 1024, 384], P('expert', 'dp')
- grad_up: bfloat16 [8, 1024, 384], P('expert', 'dp')
- grad_down: bfloat16 [8, 384, 1024], P('expert')
Inputs may be any that keep to these rules, and one draw needn't show every extreme that they name: `routes`: each row names 8 different experts. `hot_experts`: 4 different experts, all below 4. `extra_slots`: one of the entries equals 4.
All inputs are finite; a program needn't handle non-finite values.
Results may differ from a plain program's by a relative error of at most 0.0064.
Values may be sent and summed in bfloat16 or wider, within the bound.
A program may use at most 64 MiB of HBM per device.

v0:
```python
import jax
import jax.numpy as jnp
from jax import lax
from jax.sharding import PartitionSpec as P


def forward_rows(weight_gate, weight_up, weight_down, row_tokens, row_cotan, row_weights):
    gate_pre = jnp.dot(row_tokens, weight_gate, preferred_element_type=jnp.float32)
    up_proj = jnp.dot(row_tokens, weight_up, preferred_element_type=jnp.float32)
    sigmoid_gate = jax.nn.sigmoid(gate_pre)
    gate_act = gate_pre * sigmoid_gate
    hidden = (gate_act * up_proj).astype(jnp.bfloat16)
    out_grad = (row_weights.astype(jnp.float32)[:, None] * row_cotan.astype(jnp.float32)).astype(
        jnp.bfloat16
    )
    hidden_grad = jnp.dot(out_grad, weight_down.T, preferred_element_type=jnp.float32)
    gate_grad = (
        hidden_grad * up_proj * sigmoid_gate * (1.0 + gate_pre * (1.0 - sigmoid_gate))
    ).astype(jnp.bfloat16)
    up_grad = (hidden_grad * gate_act).astype(jnp.bfloat16)
    row_grads = jnp.dot(gate_grad, weight_gate.T, preferred_element_type=jnp.float32)
    row_grads = row_grads + jnp.dot(up_grad, weight_up.T, preferred_element_type=jnp.float32)
    return (row_grads.astype(jnp.bfloat16), (row_tokens, gate_grad, up_grad, hidden, out_grad))


def weight_terms(pieces):
    row_tokens, gate_grad, up_grad, hidden, out_grad = pieces
    grad_gate = jnp.dot(row_tokens.T, gate_grad, preferred_element_type=jnp.float32)
    grad_up = jnp.dot(row_tokens.T, up_grad, preferred_element_type=jnp.float32)
    grad_down = jnp.dot(hidden.T, out_grad, preferred_element_type=jnp.float32)
    return (grad_gate, grad_up, grad_down)


def expert_pass(weight_gate, weight_up, weight_down, row_tokens, row_cotan, row_weights):
    row_grads, pieces = forward_rows(
        weight_gate, weight_up, weight_down, row_tokens, row_cotan, row_weights
    )
    return (row_grads, weight_terms(pieces))


def shards(tokens, cotangent, routes, combine, hot_experts, extra_slots, w_gate, w_up, w_down):
    expert_count = lax.axis_size("expert")
    token_count, features = tokens.shape
    route_count = routes.shape[1]
    capacity = max(2, min(token_count * route_count * 7 // (8 * expert_count), token_count // 2))
    spare_slots = 2 * max(1, capacity // 6)
    expert_ids = routes.reshape(-1)
    assign_count = expert_ids.shape[0]
    assign_order = jnp.arange(assign_count, dtype=jnp.int32)
    earlier = (expert_ids[:, None] == expert_ids[None, :]) & (
        assign_order[None, :] < assign_order[:, None]
    )
    slot_rank = jnp.sum(earlier.astype(jnp.int32), axis=1)
    hot_match = expert_ids[:, None] == hot_experts[None, :]
    slot_limit = capacity + jnp.sum(jnp.where(hot_match, extra_slots[None, :], 0), axis=1)
    is_kept = slot_rank < slot_limit
    slot_count = capacity + spare_slots
    total_slots = expert_count * slot_count
    flat_slot = jnp.where(is_kept, expert_ids * slot_count + slot_rank, total_slots)
    slot_ids = jnp.arange(total_slots, dtype=jnp.int32)
    assign_onehot = slot_ids[:, None] == flat_slot[None, :]
    token_onehot = jnp.any(
        assign_onehot.reshape(total_slots, token_count, route_count), axis=2
    ).astype(jnp.bfloat16)
    both_rows = jnp.concatenate([tokens, cotangent], axis=1)
    filled = jnp.dot(token_onehot, both_rows, preferred_element_type=jnp.float32).astype(
        jnp.bfloat16
    )
    token_send = filled[:, :features].reshape(expert_count, slot_count, features)
    cotan_send = filled[:, features:].reshape(expert_count, slot_count, features)
    weight_flat = jnp.sum(
        jnp.where(assign_onehot, combine.reshape(-1).astype(jnp.float32)[None, :], 0.0), axis=1
    )
    weight_send = weight_flat.astype(jnp.bfloat16).reshape(expert_count, slot_count)
    token_recv, cotan_recv, weight_recv = (
        lax.all_to_all(token_send, "expert", split_axis=0, concat_axis=0, tiled=True),
        lax.all_to_all(cotan_send, "expert", split_axis=0, concat_axis=0, tiled=True),
        lax.all_to_all(weight_send, "expert", split_axis=0, concat_axis=0, tiled=True),
    )
    own_weights = (w_gate[0], w_up[0], w_down[0])
    all_rows, grad_terms = expert_pass(
        own_weights[0],
        own_weights[1],
        own_weights[2],
        token_recv.reshape(-1, features),
        cotan_recv.reshape(-1, features),
        weight_recv.reshape(-1),
    )
    grad_rows = all_rows.reshape(expert_count, slot_count, features)
    returned_rows = lax.all_to_all(grad_rows, "expert", split_axis=0, concat_axis=0, tiled=True)
    token_grads = jnp.dot(
        token_onehot.T,
        returned_rows.reshape(total_slots, features),
        preferred_element_type=jnp.float32,
    ).astype(jnp.bfloat16)
    grad_gate, grad_up = (
        lax.psum_scatter(grad_terms[0][None], "dp", scatter_dimension=1, tiled=True),
        lax.psum_scatter(grad_terms[1][None], "dp", scatter_dimension=1, tiled=True),
    )
    grad_down = lax.psum(grad_terms[2][None], "dp")
    return (
        token_grads,
        grad_gate.astype(jnp.bfloat16),
        grad_up.astype(jnp.bfloat16),
        grad_down.astype(jnp.bfloat16),
    )


def solution(mesh):
    in_specs = (
        P(("dp", "expert"), None),
        P(("dp", "expert"), None),
        P(("dp", "expert"), None),
        P(("dp", "expert"), None),
        P(),
        P(),
        P("expert", None, None),
        P("expert", None, None),
        P("expert", None, None),
    )
    out_specs = (
        P(("dp", "expert"), None),
        P("expert", "dp", None),
        P("expert", "dp", None),
        P("expert", None, None),
    )
    return jax.shard_map(shards, mesh=mesh, in_specs=in_specs, out_specs=out_specs, check_vma=False)
```

profile of v0, /device:TPU:0, one launch (start us, length us, event | category | flops | bytes accessed | tf_op | source)
XLA Modules:
  0.0 155.9 jit_solution(16793875699837294183)
XLA Ops:
  7.2 0.0 copy-start
  7.2 0.8 copy.24
  8.0 0.1 eq.49
  8.1 0.2 convert_reduce_fusion
  8.3 0.8 copy.26
  9.1 0.1 reshape.103
  9.1 0.8 select_reduce_fusion.1
  9.9 0.1 select_reduce_fusion
  10.0 0.7 convert_element_type.116
  10.7 6.4 %all-to-all-start = ((bf16[8,1,20]{2,1,0:T(2,128)(2,1)}), bf16[8,1,20]{2,1,0:T(2,128)(2,1)S(1)}, u32[]{:S(2)}, u32[]{:S(2)}) async-start(bf16[8,1,20]{2,1,0:T(2,128)(2,1)} %convert_element_type.116), calls=%async_computation | async-start | bytes 8192 | tf_op jit(solution)/shard_map/all_to_all | solution.py:78
  17.1 0.1 reduce_sum.30
  17.2 0.1 add.41
  17.3 0.2 fusion.11
  17.4 1.2 convolution_convert_fusion
  18.7 0.8 reshape.99
  19.5 3.0 %all-to-all-done = bf16[8,1,20]{2,1,0:T(2,128)(2,1)S(1)} async-done(((bf16[8,1,20]{2,1,0:T(2,128)(2,1)}), bf16[8,1,20]{2,1,0:T(2,128)(2,1)S(1)}, u32[]{:S(2)}, u32[]{:S(2)}) %all-to-all-start) | async-done | bytes 352 | tf_op jit(solution)/shard_map/all_to_all | solution.py:78
  22.6 3.5 %all-to-all-start.2 = ((bf16[8,20,1024]{2,1,0:T(8,128)(2,1)}), bf16[8,20,1024]{2,1,0:T(8,128)(2,1)S(1)}, u32[]{:S(2)}, u32[]{:S(2)}) async-start(bf16[8,20,1024]{2,1,0:T(8,128)(2,1)} %reshape.99), calls=%async_computation.2 | async-start | bytes 786432 | tf_op jit(solution)/shard_map/all_to_all | solution.py:76
  26.1 0.8 reshape.98
  26.9 0.0 copy-start.1
  26.9 11.6 %all-to-all-done.2 = bf16[8,20,1024]{2,1,0:T(8,128)(2,1)S(1)} async-done(((bf16[8,20,1024]{2,1,0:T(8,128)(2,1)}), bf16[8,20,1024]{2,1,0:T(8,128)(2,1)S(1)}, u32[]{:S(2)}, u32[]{:S(2)}) %all-to-all-start.2) | async-done | bytes 327712 | tf_op jit(solution)/shard_map/all_to_all | solution.py:76
  38.5 3.5 %all-to-all-start.1 = ((bf16[8,20,1024]{2,1,0:T(8,128)(2,1)}), bf16[8,20,1024]{2,1,0:T(8,128)(2,1)S(1)}, u32[]{:S(2)}, u32[]{:S(2)}) async-start(bf16[8,20,1024]{2,1,0:T(8,128)(2,1)} %reshape.98), calls=%async_computation.1 | async-start | bytes 786432 | tf_op jit(solution)/shard_map/all_to_all | solution.py:77
  42.0 0.0 reduce-scatter.3.cloned.1.call-start
  42.0 0.1 reshape.100
  42.1 0.0 copy-done
  42.1 0.3 fusion.3
  42.4 0.0 copy-done.1
  42.5 0.0 copy-start.2
  42.5 0.3 fusion.6
  42.8 0.0 copy-start.3
  42.8 11.6 %all-to-all-done.1 = bf16[8,20,1024]{2,1,0:T(8,128)(2,1)S(1)} async-done(((bf16[8,20,1024]{2,1,0:T(8,128)(2,1)}), bf16[8,20,1024]{2,1,0:T(8,128)(2,1)S(1)}, u32[]{:S(2)}, u32[]{:S(2)}) %all-to-all-start.1) | async-done | bytes 327712 | tf_op jit(solution)/shard_map/all_to_all | solution.py:77
  54.4 0.1 multiply_convert_fusion
  54.5 0.1 convert_element_type.98
  54.6 1.6 multiply_convert_fusion.4
  56.2 1.6 %convolution_bitcast_fusion.2 = f32[1,1024,384]{2,1,0:T(8,128)} fusion(bf16[160,1024]{1,0:T(8,128)(2,1)S(1)} %reshape.100, bf16[160,384]{1,0:T(8,128)(2,1)S(1)} %get-tuple-element.7), kind=kOutput, calls=%fused_computation.3 | convolution fusion | flops 125829120 | bytes 2023424 | tf_op jit(solution)/shard_map/dot_general | solution.py:28
  57.8 0.0 reduce-scatter.3.cloned.1.call-update
  57.8 0.0 reduce-scatter.5.cloned.1.call-start
  57.9 1.6 %convolution_bitcast_fusion.1 = f32[1,1024,384]{2,1,0:T(8,128)} fusion(bf16[160,1024]{1,0:T(8,128)(2,1)S(1)} %reshape.100, bf16[160,384]{1,0:T(8,128)(2,1)S(1)} %get-tuple-element.6), kind=kOutput, calls=%fused_computation.2 | convolution fusion | flops 125829120 | bytes 2023424 | tf_op jit(solution)/shard_map/dot_general | solution.py:29
  59.5 0.0 copy-done.2
  59.5 0.0 copy-done.3
  59.5 0.0 reduce-scatter.5.cloned.1.call-update
  59.6 0.1 reshape.105
  59.6 0.4 fusion.1
  60.1 0.4 fusion
  60.5 0.8 reshape.101
  61.3 3.5 %all-to-all-start.3 = ((bf16[8,20,1024]{2,1,0:T(8,128)(2,1)}), bf16[8,20,1024]{2,1,0:T(8,128)(2,1)S(1)}, u32[]{:S(2)}, u32[]{:S(2)}) async-start(bf16[8,20,1024]{2,1,0:T(8,128)(2,1)} %reshape.101), calls=%async_computation.3 | async-start | bytes 786432 | tf_op jit(solution)/shard_map/all_to_all | solution.py:90
  64.7 0.1 reshape.106
  64.8 1.5 convolution_bitcast_fusion
  66.3 78.5 %all-reduce.1 = bf16[1,384,1024]{2,1,0:T(8,128)(2,1)} all-reduce(f32[1,384,1024]{2,1,0:T(8,128)S(1)} %convolution_bitcast_fusion), channel_id=1, replica_groups=mesh['dp'=4,'expert'=8] {'dp'}, use_global_device_ids=true, to_apply=%region_6.7 | all-reduce | flops 393216 | bytes 2359296 | tf_op jit(solution)/shard_map/psum | solution.py:100
  144.8 0.0 all-to-all-done.3
  144.8 0.1 reshape.102
  144.9 0.8 convolution_convert_fusion.1
  145.7 0.0 reduce-scatter.3.cloned.1.call-done
  145.7 1.7 %convert_element_type.103 = bf16[1,256,384]{2,1,0:T(8,128)(2,1)} convert(f32[1,256,384]{2,1,0:T(8,128)} %reduce-scatter.3.cloned.1.call-done) | non-fusion elementwise | flops 98304 | bytes 589824 | tf_op jit(solution)/shard_map/convert_element_type | solution.py:103
  147.4 0.0 reduce-scatter.5.cloned.1.call-done
  147.4 1.7 %convert_element_type.104 = bf16[1,256,384]{2,1,0:T(8,128)(2,1)} convert(f32[1,256,384]{2,1,0:T(8,128)} %reduce-scatter.5.cloned.1.call-done) | non-fusion elementwise | flops 98304 | bytes 589824 | tf_op jit(solution)/shard_map/convert_element_type | solution.py:104
  (5 shorter events, 0.1 us)
Async XLA Ops:
  7.2 34.9 %copy-start = (bf16[1,1024,384]{2,1,0:T(8,128)(2,1)S(1)}, bf16[1,1024,384]{2,1,0:T(8,128)(2,1)}, u32[]{:S(2)}) copy-start(bf16[1,1024,384]{2,1,0:T(8,128)(2,1)} %param.15) | copy-start | bytes 2359300
  10.7 11.9 %all-to-all-start = ((bf16[8,1,20]{2,1,0:T(2,128)(2,1)}), bf16[8,1,20]{2,1,0:T(2,128)(2,1)S(1)}, u32[]{:S(2)}, u32[]{:S(2)}) async-start(bf16[8,1,20]{2,1,0:T(2,128)(2,1)} %convert_element_type.116), calls=%async_computation | async-start | bytes 8192 | tf_op jit(solution)/shard_map/all_to_all | solution.py:78
  22.6 15.9 %all-to-all-start.2 = ((bf16[8,20,1024]{2,1,0:T(8,128)(2,1)}), bf16[8,20,1024]{2,1,0:T(8,128)(2,1)S(1)}, u32[]{:S(2)}, u32[]{:S(2)}) async-start(bf16[8,20,1024]{2,1,0:T(8,128)(2,1)} %reshape.99), calls=%async_computation.2 | async-start | bytes 786432 | tf_op jit(solution)/shard_map/all_to_all | solution.py:76
  26.9 15.6 %copy-start.1 = (bf16[1,1024,384]{2,1,0:T(8,128)(2,1)S(1)}, bf16[1,1024,384]{2,1,0:T(8,128)(2,1)}, u32[]{:S(2)}) copy-start(bf16[1,1024,384]{2,1,0:T(8,128)(2,1)} %param.16) | copy-start | bytes 2359300
  38.5 15.9 %all-to-all-start.1 = ((bf16[8,20,1024]{2,1,0:T(8,128)(2,1)}), bf16[8,20,1024]{2,1,0:T(8,128)(2,1)S(1)}, u32[]{:S(2)}, u32[]{:S(2)}) async-start(bf16[8,20,1024]{2,1,0:T(8,128)(2,1)} %reshape.98), calls=%async_computation.1 | async-start | bytes 786432 | tf_op jit(solution)/shard_map/all_to_all | solution.py:77
  42.0 103.7 %reduce-scatter.3.cloned.1.call-start = ((), (), s32[]{:S(2)}) async-start(), calls=%async_computation.6 | async-start | bytes 1966080 | tf_op jit(solution)/shard_map/reduce_scatter | solution.py:97
  42.5 17.1 %copy-start.2 = (f32[160,384]{1,0:T(8,128)}, f32[160,384]{1,0:T(8,128)S(1)}, u32[]{:S(2)}) copy-start(f32[160,384]{1,0:T(8,128)S(1)} %fusion.3) | copy-start | bytes 737284
  42.8 16.7 %copy-start.3 = (f32[160,384]{1,0:T(8,128)}, f32[160,384]{1,0:T(8,128)S(1)}, u32[]{:S(2)}) copy-start(f32[160,384]{1,0:T(8,128)S(1)} %fusion.6) | copy-start | bytes 737284
  57.8 89.6 %reduce-scatter.5.cloned.1.call-start = ((), (), s32[]{:S(2)}) async-start(), calls=%async_computation.7 | async-start | bytes 1966080 | tf_op jit(solution)/shard_map/reduce_scatter | solution.py:98
  61.3 83.5 %all-to-all-start.3 = ((bf16[8,20,1024]{2,1,0:T(8,128)(2,1)}), bf16[8,20,1024]{2,1,0:T(8,128)(2,1)S(1)}, u32[]{:S(2)}, u32[]{:S(2)}) async-start(bf16[8,20,1024]{2,1,0:T(8,128)(2,1)} %reshape.101), calls=%async_computation.3 | async-start | bytes 786432 | tf_op jit(solution)/shard_map/all_to_all | solution.py:90
Sparse Core Ops, SparseCore 0:
  57.9 36.4 reduce-scatter.2
  97.4 43.6 reduce-scatter.4
where the time goes:
time: 157 us; the launch traced here: 156 us
  blocking collectives  78.5 us (50%)
  waiting for transfers between devices  26.3 us (17%)
  starting transfers between devices  16.8 us (11%)
  between operations  14.2 us (9%)
  matrix products  9.84 us (6%)
  local copies, waits for them, and re-layouts  5.47 us (3%)
  other arithmetic  4.81 us (3%)
    psum x1, blocking collectives, shards(): grad_down = lax.psum(grad_terms[2][None], 'dp')  78.5 us
    all_to_all x1, waiting for transfers between devices, shards(): lax.all_to_all(token_send, 'expert', split_axis=0, concat_axis=0, tiled=T...  11.6 us
    all_to_all x1, waiting for transfers between devices, shards(): lax.all_to_all(cotan_send, 'expert', split_axis=0, concat_axis=0, tiled=T...  11.6 us
    all_to_all x1, starting transfers between devices, shards(): lax.all_to_all(weight_send, 'expert', split_axis=0, concat_axis=0, tiled=...  6.35 us
    all_to_all x1, starting transfers between devices, shards(): lax.all_to_all(grad_rows, 'expert', split_axis=0, concat_axis=0, tiled=True)  3.46 us
    all_to_all x1, starting transfers between devices, shards(): lax.all_to_all(token_send, 'expert', split_axis=0, concat_axis=0, tiled=T...  3.45 us
    all_to_all x1, starting transfers between devices, shards(): lax.all_to_all(cotan_send, 'expert', split_axis=0, concat_axis=0, tiled=T...  3.45 us
  transfers between devices with their start and end apart: 6, of which 3 were waited for; matrix products, arithmetic and copies ran while one was open for 7% of the time, Pallas kernels for 0%

commit v1 on v0

--- a/solution.py
+++ b/solution.py
@@ -2,6 +2,18 @@
 import jax.numpy as jnp
 from jax import lax
 from jax.sharding import PartitionSpec as P
+
+
+def create_routes_all(sheet, lane_axis):
+    top, d_next = (sheet, 0)
+    degree = lax.axis_size(lane_axis)
+    while 1 << d_next < degree:
+        a_next = lax.ppermute(
+            top, axis_name=lane_axis, perm=list(map(lambda p: (p, p ^ 1 << d_next), range(degree)))
+        )
+        top = top + a_next
+        d_next = d_next + 1
+    return top
 
 
 def forward_rows(weight_gate, weight_up, weight_down, row_tokens, row_cotan, row_weights):
@@ -97,7 +109,7 @@
         lax.psum_scatter(grad_terms[0][None], "dp", scatter_dimension=1, tiled=True),
         lax.psum_scatter(grad_terms[1][None], "dp", scatter_dimension=1, tiled=True),
     )
-    grad_down = lax.psum(grad_terms[2][None], "dp")
+    grad_down = create_routes_all(grad_terms[2][None], "dp")
     return (
         token_grads,
         grad_gate.astype(jnp.bfloat16),

time: 157 us -> 170 us (1.083)
  waiting for transfers between devices: 26.3 us -> 96.4 us
  blocking collectives: 78.5 us -> 15.6 us
  other arithmetic: 4.81 us -> 10.8 us
    psum x1 -> x0, blocking collectives: 78.5 us -> none  [shards(): grad_down = lax.psum(grad_terms[2][None], 'dp')]
    ppermute x0 -> x2, waiting for transfers between devices: none -> 55.6 us  [create_routes_all(): lax.ppermute(top, axis_name=lane_axis, perm=list(map(lambda p: (p, p ^ 1...]
    all_to_all x0 -> x1, blocking collectives: none -> 15.6 us  [shards(): lax.all_to_all(grad_rows, 'expert', split_axis=0, concat_axis=0, tiled=True)]
    reduce_scatter x1, waiting for transfers between devices: 0.01 us -> 13.9 us  [shards(): lax.psum_scatter(grad_terms[0][None], 'dp', scatter_dimension=1, tiled=True)]
    all_to_all x1 -> x0, starting transfers between devices: 3.46 us -> none  [shards(): lax.all_to_all(grad_rows, 'expert', split_axis=0, concat_axis=0, tiled=True)]
    add x0 -> x1, other arithmetic: none -> 3.06 us  [create_routes_all(): top = top + a_next]
    convert_element_type x0 -> x1, other arithmetic: none -> 2.98 us  [shards(): grad_down.astype(jnp.bfloat16)]
    ppermute x0 -> x2, starting transfers between devices: none -> 2.88 us  [create_routes_all(): lax.ppermute(top, axis_name=lane_axis, perm=list(map(lambda p: (p, p ^ 1...]
  transfers between devices with their start and end apart: 6 -> 7, of which waited for: 3 -> 6; matrix products, arithmetic and copies ran while one was open for 7% -> 10% of each run, Pallas kernels for 0% -> 0%
where the time goes in v1:
time: 170 us; the launch traced here: 169 us
  waiting for transfers between devices  96.4 us (57%)
  starting transfers between devices  16.2 us (10%)
  blocking collectives  15.6 us (9%)
  between operations  14.2 us (8%)
  other arithmetic  10.8 us (6%)
  matrix products  9.63 us (6%)
  local copies, waits for them, and re-layouts  6.02 us (4%)
    ppermute x2, waiting for transfers between devices, create_routes_all(): lax.ppermute(top, axis_name=lane_axis, perm=list(map(lambda p: (p, p ^ 1...  55.6 us
    all_to_all x1, blocking collectives, shards(): lax.all_to_all(grad_rows, 'expert', split_axis=0, concat_axis=0, tiled=True)  15.6 us
    reduce_scatter x1, waiting for transfers between devices, shards(): lax.psum_scatter(grad_terms[0][None], 'dp', scatter_dimension=1, tiled=True)  13.9 us
    all_to_all x1, waiting for transfers between devices, shards(): lax.all_to_all(token_send, 'expert', split_axis=0, concat_axis=0, tiled=T...  12.2 us
    all_to_all x1, waiting for transfers between devices, shards(): lax.all_to_all(cotan_send, 'expert', split_axis=0, concat_axis=0, tiled=T...  11.6 us
    all_to_all x1, starting transfers between devices, shards(): lax.all_to_all(weight_send, 'expert', split_axis=0, concat_axis=0, tiled=...  6.35 us
    all_to_all x1, starting transfers between devices, shards(): lax.all_to_all(token_send, 'expert', split_axis=0, concat_axis=0, tiled=T...  3.45 us
    all_to_all x1, starting transfers between devices, shards(): lax.all_to_all(cotan_send, 'expert', split_axis=0, concat_axis=0, tiled=T...  3.45 us
  transfers between devices with their start and end apart: 7, of which 6 were waited for; matrix products, arithmetic and copies ran while one was open for 10% of the time, Pallas kernels for 0%

profile of v1, /device:TPU:0, one launch (start us, length us, event | category | flops | bytes accessed | tf_op | source)
XLA Modules:
  0.0 168.9 jit_solution(3490447555295745100)
XLA Ops:
  7.2 0.0 copy-start
  7.2 0.8 copy.24
  8.0 0.1 eq.49
  8.1 0.2 convert_reduce_fusion
  8.3 0.8 copy.26
  9.1 0.1 reshape.103
  9.1 0.8 select_reduce_fusion.1
  9.9 0.1 select_reduce_fusion
  10.0 0.7 convert_element_type.116
  10.7 6.4 %all-to-all-start = ((bf16[8,1,20]{2,1,0:T(2,128)(2,1)}), bf16[8,1,20]{2,1,0:T(2,128)(2,1)S(1)}, u32[]{:S(2)}, u32[]{:S(2)}) async-start(bf16[8,1,20]{2,1,0:T(2,128)(2,1)} %convert_element_type.116), calls=%async_computation | async-start | bytes 8192 | tf_op jit(solution)/shard_map/all_to_all | solution.py:90
  17.1 0.1 reduce_sum.30
  17.2 0.1 add.45
  17.3 0.2 fusion.11
  17.4 1.2 convolution_convert_fusion
  18.7 0.8 reshape.98
  19.5 3.0 %all-to-all-done = bf16[8,1,20]{2,1,0:T(2,128)(2,1)S(1)} async-done(((bf16[8,1,20]{2,1,0:T(2,128)(2,1)}), bf16[8,1,20]{2,1,0:T(2,128)(2,1)S(1)}, u32[]{:S(2)}, u32[]{:S(2)}) %all-to-all-start) | async-done | bytes 352 | tf_op jit(solution)/shard_map/all_to_all | solution.py:90
  22.6 3.5 %all-to-all-start.1 = ((bf16[8,20,1024]{2,1,0:T(8,128)(2,1)}), bf16[8,20,1024]{2,1,0:T(8,128)(2,1)S(1)}, u32[]{:S(2)}, u32[]{:S(2)}) async-start(bf16[8,20,1024]{2,1,0:T(8,128)(2,1)} %reshape.98), calls=%async_computation.1 | async-start | bytes 786432 | tf_op jit(solution)/shard_map/all_to_all | solution.py:89
  26.0 0.8 reshape.99
  26.9 11.6 %all-to-all-done.1 = bf16[8,20,1024]{2,1,0:T(8,128)(2,1)S(1)} async-done(((bf16[8,20,1024]{2,1,0:T(8,128)(2,1)}), bf16[8,20,1024]{2,1,0:T(8,128)(2,1)S(1)}, u32[]{:S(2)}, u32[]{:S(2)}) %all-to-all-start.1) | async-done | bytes 327712 | tf_op jit(solution)/shard_map/all_to_all | solution.py:89
  38.5 3.5 %all-to-all-start.2 = ((bf16[8,20,1024]{2,1,0:T(8,128)(2,1)}), bf16[8,20,1024]{2,1,0:T(8,128)(2,1)S(1)}, u32[]{:S(2)}, u32[]{:S(2)}) async-start(bf16[8,20,1024]{2,1,0:T(8,128)(2,1)} %reshape.99), calls=%async_computation.2 | async-start | bytes 786432 | tf_op jit(solution)/shard_map/all_to_all | solution.py:88
  42.0 0.0 reduce-scatter.5.cloned.1.call-start
  42.0 0.1 multiply_convert_fusion
  42.2 0.0 copy-start.1
  42.2 0.1 convert_element_type.98
  42.2 12.2 %all-to-all-done.2 = bf16[8,20,1024]{2,1,0:T(8,128)(2,1)S(1)} async-done(((bf16[8,20,1024]{2,1,0:T(8,128)(2,1)}), bf16[8,20,1024]{2,1,0:T(8,128)(2,1)S(1)}, u32[]{:S(2)}, u32[]{:S(2)}) %all-to-all-start.2) | async-done | bytes 327712 | tf_op jit(solution)/shard_map/all_to_all | solution.py:88
  54.4 0.1 reshape.100
  54.5 0.0 copy-done
  54.5 0.0 copy-start.8
  54.5 0.3 fusion.3
  54.8 0.0 copy-done.1
  54.8 0.0 copy-start.2
  54.9 0.3 fusion.6
  55.2 0.4 copy-done.8
  55.6 1.1 multiply_convert_fusion.4
  56.7 1.6 convolution_bitcast_fusion.1
  58.3 0.0 reduce-scatter.5.cloned.1.call-update
  58.3 0.0 copy-done.6
  58.4 0.0 reduce-scatter.3.cloned.1.call-start
  58.4 0.1 reshape.105
  58.5 0.0 copy-done.2
  58.5 0.0 copy-done.3
  58.5 0.9 reshape.106
  59.4 1.8 %convolution_bitcast_fusion = f32[1,384,1024]{2,1,0:T(8,128)S(1)} fusion(f32[160,1024]{1,0:T(8,128)} %reshape.106, f32[160]{0:T(256)S(1)} %reshape.105, f32[160,384]{1,0:T(8,128)} %copy-done.3, f32[160,384]{1,0:T(8,128)} %copy-done.2), kind=kOutput, calls=%fused_computation.2 | convolution fusion | flops 126525440 | bytes 2720384 | tf_op jit(solution)/shard_map/dot_general | solution.py:42
  61.2 1.6 collective-permute-start
  62.8 0.0 copy-done.4
  62.8 1.6 convolution_bitcast_fusion.2
  64.4 0.0 reduce-scatter.3.cloned.1.call-update
  64.4 0.0 copy-start.5
  64.4 45.2 %collective-permute-done = f32[1,384,1024]{2,1,0:T(8,128)} collective-permute-done((f32[1,384,1024]{2,1,0:T(8,128)S(1)}, f32[1,384,1024]{2,1,0:T(8,128)}, u32[]{:S(2)}, u32[]{:S(2)}) %collective-permute-start) | collective-permute-done | bytes 1572896 | tf_op jit(solution)/shard_map/ppermute | solution.py:11
  109.6 3.1 %add.51 = f32[1,384,1024]{2,1,0:T(8,128)} add(f32[1,384,1024]{2,1,0:T(8,128)S(1)} %convolution_bitcast_fusion, f32[1,384,1024]{2,1,0:T(8,128)} %collective-permute-done) | non-fusion elementwise | flops 393216 | bytes 4718592 | tf_op jit(solution)/shard_map/add | solution.py:14
  112.7 1.3 collective-permute-start.1
  114.0 0.0 copy-done.5
  114.0 0.4 fusion.1
  114.4 0.0 copy-done.7
  114.4 0.4 fusion
  114.8 0.1 reshape.101
  114.9 15.6 %all_to_all.21 = bf16[8,20,1024]{2,1,0:T(8,128)(2,1)S(1)} all-to-all(bf16[8,20,1024]{2,1,0:T(8,128)(2,1)S(1)} %reshape.101), channel_id=1, replica_groups=mesh['dp'=4,'expert'=8] {'expert'}, dimensions={0} | all-to-all | bytes 655360 | tf_op jit(solution)/shard_map/all_to_all | solution.py:102
  130.5 0.1 reshape.102
  130.6 0.8 convolution_convert_fusion.1
  131.4 1.7 %convert_element_type.104 = bf16[1,256,384]{2,1,0:T(8,128)(2,1)} convert(f32[1,256,384]{2,1,0:T(8,128)} %reduce-scatter.5.cloned.1.call-done) | non-fusion elementwise | flops 98304 | bytes 589824 | tf_op jit(solution)/shard_map/convert_element_type | solution.py:116
  133.1 13.9 %reduce-scatter.3.cloned.1.call-done = f32[1,256,384]{2,1,0:T(8,128)} async-done(((f32[1,1024,384]{2,1,0:T(8,128)}), f32[1,256,384]{2,1,0:T(8,128)}) %reduce-scatter.3.cloned.1.call-update) | async-done | bytes 393232 | tf_op jit(solution)/shard_map/reduce_scatter | solution.py:109
  147.0 1.7 %convert_element_type.103 = bf16[1,256,384]{2,1,0:T(8,128)(2,1)} convert(f32[1,256,384]{2,1,0:T(8,128)} %reduce-scatter.3.cloned.1.call-done) | non-fusion elementwise | flops 98304 | bytes 589824 | tf_op jit(solution)/shard_map/convert_element_type | solution.py:115
  148.7 10.4 %collective-permute-done.1 = f32[1,384,1024]{2,1,0:T(8,128)} collective-permute-done((f32[1,384,1024]{2,1,0:T(8,128)}, f32[1,384,1024]{2,1,0:T(8,128)}, u32[]{:S(2)}, u32[]{:S(2)}) %collective-permute-start.1) | collective-permute-done | bytes 1572896 | tf_op jit(solution)/shard_map/ppermute | solution.py:11
  159.1 3.0 %add_convert_fusion = bf16[1,384,1024]{2,1,0:T(8,128)(2,1)} fusion(f32[1,384,1024]{2,1,0:T(8,128)} %add.51, f32[1,384,1024]{2,1,0:T(8,128)} %collective-permute-done.1), kind=kLoop, calls=%fused_computation.1 | loop fusion | flops 786432 | bytes 3932160 | tf_op jit(solution)/shard_map/convert_element_type | solution.py:117
  (10 shorter events, 0.1 us)
Async XLA Ops:
  7.2 47.3 %copy-start = (bf16[1,1024,384]{2,1,0:T(8,128)(2,1)S(1)}, bf16[1,1024,384]{2,1,0:T(8,128)(2,1)}, u32[]{:S(2)}) copy-start(bf16[1,1024,384]{2,1,0:T(8,128)(2,1)} %param.15) | copy-start | bytes 2359300
  10.7 11.9 %all-to-all-start = ((bf16[8,1,20]{2,1,0:T(2,128)(2,1)}), bf16[8,1,20]{2,1,0:T(2,128)(2,1)S(1)}, u32[]{:S(2)}, u32[]{:S(2)}) async-start(bf16[8,1,20]{2,1,0:T(2,128)(2,1)} %convert_element_type.116), calls=%async_computation | async-start | bytes 8192 | tf_op jit(solution)/shard_map/all_to_all | solution.py:90
  22.6 15.9 %all-to-all-start.1 = ((bf16[8,20,1024]{2,1,0:T(8,128)(2,1)}), bf16[8,20,1024]{2,1,0:T(8,128)(2,1)S(1)}, u32[]{:S(2)}, u32[]{:S(2)}) async-start(bf16[8,20,1024]{2,1,0:T(8,128)(2,1)} %reshape.98), calls=%async_computation.1 | async-start | bytes 786432 | tf_op jit(solution)/shard_map/all_to_all | solution.py:89
  38.5 15.9 %all-to-all-start.2 = ((bf16[8,20,1024]{2,1,0:T(8,128)(2,1)}), bf16[8,20,1024]{2,1,0:T(8,128)(2,1)S(1)}, u32[]{:S(2)}, u32[]{:S(2)}) async-start(bf16[8,20,1024]{2,1,0:T(8,128)(2,1)} %reshape.99), calls=%async_computation.2 | async-start | bytes 786432 | tf_op jit(solution)/shard_map/all_to_all | solution.py:88
  42.0 89.4 %reduce-scatter.5.cloned.1.call-start = ((), (), s32[]{:S(2)}) async-start(), calls=%async_computation.7 | async-start | bytes 1966080 | tf_op jit(solution)/shard_map/reduce_scatter | solution.py:110
  42.2 12.7 %copy-start.1 = (bf16[1,1024,384]{2,1,0:T(8,128)(2,1)S(1)}, bf16[1,1024,384]{2,1,0:T(8,128)(2,1)}, u32[]{:S(2)}) copy-start(bf16[1,1024,384]{2,1,0:T(8,128)(2,1)} %param.16) | copy-start | bytes 2359300
  54.5 1.1 copy-start.8
  54.8 3.7 %copy-start.2 = (f32[160,384]{1,0:T(8,128)}, f32[160,384]{1,0:T(8,128)S(1)}, u32[]{:S(2)}) copy-start(f32[160,384]{1,0:T(8,128)S(1)} %fusion.3) | copy-start | bytes 737284
  55.6 2.9 %copy-start.3 = (f32[160,384]{1,0:T(8,128)}, f32[160,384]{1,0:T(8,128)S(1)}, u32[]{:S(2)}) copy-start(f32[160,384]{1,0:T(8,128)S(1)} %fusion.6) | copy-start | bytes 737284
  56.7 1.7 copy-start.6
  58.4 88.7 %reduce-scatter.3.cloned.1.call-start = ((), (), s32[]{:S(2)}) async-start(), calls=%async_computation.6 | async-start | bytes 1966080 | tf_op jit(solution)/shard_map/reduce_scatter | solution.py:109
  59.4 3.4 %copy-start.4 = (bf16[160,384]{1,0:T(8,128)(2,1)S(1)}, bf16[160,384]{1,0:T(8,128)(2,1)}, u32[]{:S(2)}) copy-start(bf16[160,384]{1,0:T(8,128)(2,1)} %get-tuple-element.7) | copy-start | bytes 368644
  61.2 48.4 %collective-permute-start = (f32[1,384,1024]{2,1,0:T(8,128)S(1)}, f32[1,384,1024]{2,1,0:T(8,128)}, u32[]{:S(2)}, u32[]{:S(2)}) collective-permute-start(f32[1,384,1024]{2,1,0:T(8,128)S(1)} %convolution_bitcast_fusion), channel_id=1, source_target_pairs={{0,8},{8,0},{16,24},{24,16},{1,9},{9,1},{17,25},{25,17},{2,10},{10... | collective-permute-start | bytes 4718600 | tf_op jit(solution)/shard_map/ppermute | solution.py:11
  64.4 49.6 %copy-start.5 = (bf16[160,384]{1,0:T(8,128)(2,1)S(1)}, bf16[160,384]{1,0:T(8,128)(2,1)}, u32[]{:S(2)}) copy-start(bf16[160,384]{1,0:T(8,128)(2,1)} %get-tuple-element.7) | copy-start | bytes 368644
  112.7 1.7 %copy-start.7 = (bf16[160,384]{1,0:T(8,128)(2,1)S(1)}, bf16[160,384]{1,0:T(8,128)(2,1)}, u32[]{:S(2)}) copy-start(bf16[160,384]{1,0:T(8,128)(2,1)} %copy-done.6) | copy-start | bytes 368644
  112.7 46.4 %collective-permute-start.1 = (f32[1,384,1024]{2,1,0:T(8,128)}, f32[1,384,1024]{2,1,0:T(8,128)}, u32[]{:S(2)}, u32[]{:S(2)}) collective-permute-start(f32[1,384,1024]{2,1,0:T(8,128)} %add.51), channel_id=1, source_target_pairs={{0,16},{8,24},{16,0},{24,8},{1,17},{9,25},{17,1},{25,9},{2,18},{10... | collective-permute-start | bytes 4718600 | tf_op jit(solution)/shard_map/ppermute | solution.py:11
Sparse Core Ops, SparseCore 0:
  58.5 42.5 reduce-scatter.4
  104.1 42.9 reduce-scatter.2
